TPU v7x, 128 devices: a whole 4x4x4 slice. The times are simulated.
128 devices in a mesh: seq: 8 (over x, core), exp: 16 (over y, z).
Axes of the slice: x: 4, y: 4, z: 4, core: 2. Of those that a mesh axis runs over, the one named last changes fastest.
Arguments:
- xin: bfloat16 [512, 4, 8192], P('seq', None, 'exp'), may hold values from -6 to 6
- zin: bfloat16 [512, 4, 8192], P('seq', None, 'exp'), may hold values from -6 to 6
- conv_weight: float32 [4, 8192], P(None, 'exp'), may hold values from -3 to 3
- conv_bias: float32 [8192], P('exp'), may hold values from -3 to 3
- xproj_weight: bfloat16 [8192, 288], P('exp'), may hold values from -0.0625 to 0.0625
- dtproj_weight: bfloat16 [256, 8192], P(None, 'exp'), may hold values from -0.375 to 0.375
- dt_bias: float32 [8192], P('exp'), may hold values from -5 to -3
- a_log: float32 [16, 8192], P(None, 'exp'), may hold values from -3 to 1
- skip: float32 [8192], P('exp'), may hold values from 0.2 to 1
- out_weight: bfloat16 [8192, 4096], P('exp'), may hold values from -0.0625 to 0.0625
- resid: bfloat16 [512, 4, 4096], P(('seq', 'exp')), may hold values from -6 to 6
- norm_gain: float32 [4096], replicated, may hold values from 0.5 to 1.5
- expert_ids: int32 [512, 4, 2], P(('seq', 'exp')), may hold values from 0 to 7, all different within a row; in each aligned block of 16 rows (0 to 15, 16 to 31, ..., all dimensions but the last counted through in order) at most 8 rows name the same one
- gate_weights: bfloat16 [512, 4, 2], P(('seq', 'exp')), may hold values from 0.19921875 to 1
- w_gate: bfloat16 [16, 4096, 6144], P('exp', None, 'seq'), may hold values from -0.09375 to 0.09375
- w_up: bfloat16 [16, 4096, 6144], P('exp', None, 'seq'), may hold values from -0.09375 to 0.09375
- w_down: bfloat16 [16, 6144, 4096], P('exp', 'seq'), may hold values from -0.0546875 to 0.0546875
Outputs:
- layer_out: bfloat16 [512, 4, 4096], P(('seq', 'exp'))
Inputs may be any that keep to these rules, and one draw needn't show every extreme that they name: `expert_ids`: tokens are ordered by position, then document; in each aligned block of 16 such tokens (the tokens of one device), every expert is named at most 8 times, and in every draw some expert is named exactly 8 times in some block. Each token names 2 different experts.
All inputs are finite; a program needn't handle non-finite values.
Results may differ from a plain program's by a relative error of at most 0.03.
Values may be sent and summed in bfloat16 or wider, within the bound.
No kernel may reach another device: no remote copies, remote signals or barrier semaphores. Data moves between devices by JAX's collectives and lax.ppermute only.
A program may use at most 128 MiB of HBM per device.

v0:
```python
import jax
import jax.numpy as jnp
from jax import lax
from jax.sharding import PartitionSpec as P

D = 4096
STATE = 16
CONV = 4
RANK = 256
EXPERTS = 8
TOPK = 2


def passed_along(value, axis, by):
    count = lax.axis_size(axis)
    pairs = [(i, i + by) for i in range(count) if 0 <= i + by < count]
    return lax.ppermute(value, axis, pairs)


def entering(value, axis, join, neutral):
    place = lax.axis_index(axis)
    gathered = jax.tree.map(
        lambda a, kind: lax.all_gather(a.astype(kind), axis), value, (jnp.bfloat16, jnp.bfloat16)
    )
    state = jax.tree.map(lambda a, e: jnp.zeros_like(a) + jnp.asarray(e, a.dtype), value, neutral)

    def one(step, state):
        return join(
            state,
            jax.tree.map(
                lambda a, own: lax.dynamic_index_in_dim(a, step, 0, False).astype(own.dtype),
                gathered,
                value,
            ),
        )

    return lax.fori_loop(0, place, one, state)


def conv_inputs(window, conv_weight, conv_bias, length):
    running = jnp.zeros(window[:length].shape, jnp.float32) + conv_bias
    for offset in range(CONV):
        running = running + conv_weight[offset] * window[offset : offset + length]
    return running


def make_step(decay_rate):

    def advance(carry_state, series_now):
        step_now, input_now, read_now, value_now = series_now
        factor = jnp.exp(step_now[:, None, :] * decay_rate[None])
        carry_state = (
            factor * carry_state + (step_now * value_now)[:, None, :] * input_now[:, :, None]
        )
        return (carry_state, jnp.sum(read_now[:, :, None] * carry_state, axis=1))

    return advance


def chain(earlier, later):
    return (earlier[0] * later[0], later[0] * earlier[1] + later[1])


def slot_select(route_ids, capacity):
    flat_ids = route_ids.reshape(-1)
    onehot = (flat_ids[:, None] == jnp.arange(EXPERTS, dtype=jnp.int32)[None, :]).astype(jnp.int32)
    before = jnp.sum((jnp.cumsum(onehot, axis=0) - onehot) * onehot, axis=1)
    target = flat_ids * capacity + before
    matches = jnp.arange(EXPERTS * capacity, dtype=jnp.int32)[:, None] == target[None, :]
    return matches.reshape(EXPERTS * capacity, route_ids.shape[0], route_ids.shape[1])


def per_device(
    xin,
    zin,
    conv_weight,
    conv_bias,
    xproj_weight,
    dtproj_weight,
    dt_bias,
    a_log,
    skip,
    out_weight,
    resid,
    norm_gain,
    expert_ids,
    gate_weights,
    w_gate,
    w_up,
    w_down,
):
    section = xin.shape[0]
    edge_rows = passed_along(xin[section - (CONV - 1) :], "seq", 1)
    window = jnp.concatenate([edge_rows, xin], axis=0).astype(jnp.float32)
    inner_act = jax.nn.silu(conv_inputs(window, conv_weight, conv_bias, section)).astype(
        jnp.bfloat16
    )
    inner_f = inner_act.astype(jnp.float32)
    projected = jnp.einsum(
        "pbc,cr->pbr", inner_act, xproj_weight, preferred_element_type=jnp.float32
    )
    projected = lax.psum(projected.astype(jnp.bfloat16), "exp").astype(jnp.float32)
    low_rank = projected[..., :RANK].astype(jnp.bfloat16)
    in_state = projected[..., RANK : RANK + STATE]
    out_state = projected[..., RANK + STATE :]
    step_size = jax.nn.softplus(
        jnp.einsum("pbr,rc->pbc", low_rank, dtproj_weight, preferred_element_type=jnp.float32)
        + dt_bias
    )
    decay_rate = -jnp.exp(a_log)
    advance = make_step(decay_rate)
    series = (step_size, in_state, out_state, inner_f)
    zero_state = jnp.zeros((xin.shape[1], STATE, xin.shape[2]), jnp.float32)
    final_local, local_out = lax.scan(advance, zero_state, series)
    total_decay = jnp.exp(jnp.sum(step_size, axis=0)[:, None, :] * decay_rate[None])
    identity = (jnp.ones_like(total_decay), jnp.zeros_like(final_local))
    incoming = entering((total_decay, final_local), "seq", chain, identity)[1]
    ignored, ssm_out = lax.scan(advance, incoming, series)
    mixed_in = ((ssm_out + skip * inner_f) * jax.nn.silu(zin.astype(jnp.float32))).astype(
        jnp.bfloat16
    )
    row_block = mixed_in
    mamba_rows = lax.psum_scatter(
        jnp.einsum("pbc,cd->pbd", row_block, out_weight, preferred_element_type=jnp.float32).astype(
            jnp.bfloat16
        ),
        "exp",
        scatter_dimension=0,
        tiled=True,
    ).astype(jnp.float32)
    hidden_state = resid.astype(jnp.float32) + mamba_rows
    norm_scale = lax.rsqrt(jnp.mean(hidden_state * hidden_state, axis=-1, keepdims=True) + 1e-05)
    normed = (hidden_state * norm_scale * norm_gain).astype(jnp.bfloat16)
    row_count = resid.shape[0] * resid.shape[1]
    capacity = 2 * TOPK * row_count // EXPERTS
    splits = lax.axis_size("exp") // EXPERTS
    tokens = normed.reshape(row_count, D)
    route_ids = expert_ids.reshape(row_count, TOPK)
    gate_vals = gate_weights.reshape(row_count, TOPK)
    matches = slot_select(route_ids, capacity)
    chosen = jnp.sum(matches.astype(jnp.int32), axis=2).astype(jnp.bfloat16)
    outgoing = (
        jnp.dot(chosen, tokens, preferred_element_type=jnp.float32)
        .astype(jnp.bfloat16)
        .reshape(EXPERTS, capacity, D)
    )
    arrived = lax.all_to_all(
        jnp.tile(outgoing, (splits, 1, 1)), "exp", split_axis=0, concat_axis=0, tiled=True
    )
    everything = lax.all_gather(arrived, "seq", axis=0, tiled=True)
    row_block = everything
    expert_row_block = row_block.reshape(-1, D)
    gate_act = jnp.dot(expert_row_block, w_gate[0], preferred_element_type=jnp.float32)
    up_act = jnp.dot(expert_row_block, w_up[0], preferred_element_type=jnp.float32)
    hidden = (jax.nn.silu(gate_act) * up_act).astype(jnp.bfloat16)
    own_rows = lax.psum_scatter(
        jnp.dot(hidden, w_down[0], preferred_element_type=jnp.float32)
        .reshape(lax.axis_size("seq") * arrived.shape[0], capacity, D)
        .astype(jnp.bfloat16),
        "seq",
        scatter_dimension=0,
        tiled=True,
    ).astype(jnp.float32)
    returned = lax.all_to_all(
        own_rows.astype(jnp.bfloat16), "exp", split_axis=0, concat_axis=0, tiled=True
    ).astype(own_rows.dtype)
    summed = jnp.sum(returned.reshape(splits, EXPERTS * capacity, D), axis=0)
    weights = jnp.sum(matches.astype(jnp.float32) * gate_vals.astype(jnp.float32)[None], axis=2)
    expert_out = jnp.dot(weights.T, summed, precision=lax.Precision.HIGHEST)
    return (hidden_state + expert_out.reshape(hidden_state.shape)).astype(jnp.bfloat16)


def solution(mesh):
    placed = (
        P("seq", None, "exp"),
        P("seq", None, "exp"),
        P(None, "exp"),
        P("exp"),
        P("exp", None),
        P(None, "exp"),
        P("exp"),
        P(None, "exp"),
        P("exp"),
        P("exp", None),
        P(("seq", "exp"), None, None),
        P(),
        P(("seq", "exp"), None, None),
        P(("seq", "exp"), None, None),
        P("exp", None, "seq"),
        P("exp", None, "seq"),
        P("exp", "seq", None),
    )
    return jax.shard_map(
        per_device,
        mesh=mesh,
        in_specs=placed,
        out_specs=P(("seq", "exp"), None, None),
        check_vma=False,
    )
```

profile of v0, /device:TPU:2, one launch (start us, length us, event | category | flops | bytes accessed | tf_op | source)
XLA Modules:
  0.0 485.4 jit_solution(7767882943626385610)
XLA Ops:
  7.4 1.9 collective-permute-start
  10.2 2.2 collective-permute-done
  12.4 1.1 maximum_convert_fusion
  13.5 1.2 fusion.39
  15.8 86.0 %all-reduce.4.cloned.1.call-done = bf16[64,4,288]{2,0,1:T(8,128)(2,1)} async-done(((bf16[64,4,288]{2,0,1:T(8,128)(2,1)}), bf16[64,4,288]{2,0,1:T(8,128)(2,1)}) %all-reduce.4.cloned.1.call-update) | async-done | bytes 147472 | tf_op jit(solution)/shard_map/psum | solution.py:102
  101.8 1.2 fusion.35
  103.6 1.7 fusion.42
  105.4 10.3 %while.37 = (s32[]{:T(128)}, f32[4,16,512]{2,1,0:T(8,128)S(1)}, f32[64,4,512]{2,1,0:T(4,128)S(1)}, f32[16,512]{1,0:T(8,128)S(1)}, f32[64,4,512]{2,1,0:T(4,128)S(...) while((s32[]{:T(128)}, f32[4,16,512]{2,1,0:T(8,128)S(1)}, f32[64,4,512]{2,1,0:T(4,128)S(1)}, ...), condition=%wide.region_3.4_spmd.clone, body=%wide.region_2.3_spmd.clone.sunk | while | flops 165891 | bytes 353131 | solution.py:114
  115.7 13.1 %all-gather = bf16[32,16,512]{2,1,0:T(8,128)(2,1)S(1)} all-gather(bf16[4,16,512]{2,1,0:T(8,128)(2,1)S(1)} %convert_element_type.103), channel_id=2, replica_groups=mesh['seq'=8,'exp'=16] {'seq'}, dimensions={0}, use_global_device_ids=true | all-gather | bytes 589824 | tf_op jit(solution)/shard_map/all_gather | solution.py:23
  128.9 13.1 %all_gather.13 = bf16[8,4,16,512]{3,2,1,0:T(8,128)(2,1)S(1)} all-gather(bf16[1,4,16,512]{3,2,1,0:T(8,128)(2,1)S(1)} %exponential_convert_fusion), channel_id=1, replica_groups=mesh['seq'=8,'exp'=16] {'seq'}, dimensions={0}, use_global_device_ids=true | all-gather | bytes 589824 | tf_op jit(solution)/shard_map/all_gather | solution.py:23
  142.2 58.7 %while.36 = (s32[]{:T(128)}, f32[4,16,512]{2,1,0:T(8,128)S(1)}, f32[64,4,512]{2,1,0:T(4,128)S(1)}, f32[64,4,512]{2,1,0:T(4,128)S(1)}, f32[16,512]{1,0:T(8,128)S(...) while((s32[]{:T(128)}, f32[4,16,512]{2,1,0:T(8,128)S(1)}, ...), condition=%wide.region_8.9_spmd, body=%wide.region_6.8_spmd.sunk | while | flops 196610 | bytes 378481 | solution.py:118
  200.9 1.3 fusion.30
  202.3 4.8 convolution_convert_fusion.1
  209.3 87.8 %all-reduce.6.cloned.1.call-done = bf16[64,4,4096]{2,0,1:T(8,128)(2,1)} async-done(((bf16[64,4,4096]{2,0,1:T(8,128)(2,1)}), bf16[64,4,4096]{2,0,1:T(8,128)(2,1)}) %all-reduce.6.cloned.1.call-update) | async-done | bytes 2097168
  299.1 20.6 %all_to_all.10 = bf16[16,8,4096]{2,1,0:T(8,128)(2,1)} all-to-all(bf16[16,8,4096]{2,1,0:T(8,128)(2,1)S(1)} %bitcast.113), channel_id=1, replica_groups=mesh['seq'=8,'exp'=16] {'exp'}, dimensions={0} | all-to-all | bytes 2097152 | tf_op jit(solution)/shard_map/all_to_all | solution.py:147
  319.9 46.7 %all-gather.3.cloned.1.call-done = bf16[128,8,4096]{2,1,0:T(8,128)(2,1)} async-done(((bf16[16,8,4096]{2,1,0:T(8,128)(2,1)}), bf16[128,8,4096]{2,1,0:T(8,128)(2,1)}) %all-gather.3.cloned.1.call-update) | async-done | bytes 8388624 | tf_op jit(solution)/shard_map/all_gather | solution.py:150
  366.6 11.0 %fusion.1 = f32[1024,768]{1,0:T(8,128)S(1)} fusion(bf16[128,8,4096]{2,1,0:T(8,128)(2,1)} %all-gather.3.cloned.1.call-done, bf16[1,4096,768]{2,1,0:T(8,128)(2,1)} %param.38), kind=kOutput, calls=%fused_computation.14 | convolution fusion | flops 6442450944 | bytes 17825792 | tf_op jit(solution)/shard_map/dot_general | solution.py:154
  377.7 9.9 %fusion.16 = bf16[128,8,768]{2,1,0:T(8,128)(2,1)S(1)} fusion(f32[1024,768]{1,0:T(8,128)S(1)} %fusion.1, bf16[1,4096,768]{2,1,0:T(8,128)(2,1)} %param.37, bf16[128,8,4096]{2,1,0:T(8,128)(2,1)S(1)} %copy-done.9), kind=kOutput, calls=%fused_computation.31 | convolution fusion | flops 6447169536 | bytes 19398656 | tf_op jit(solution)/shard_map/dot_general | solution.py:153
  387.6 8.9 %convolution_convert_fusion = bf16[128,8,4096]{2,0,1:T(8,128)(2,1)} fusion(bf16[1,768,4096]{2,1,0:T(8,128)(2,1)S(1)} %bitcast.122, bf16[128,8,768]{2,1,0:T(8,128)(2,1)S(1)} %fusion.16), kind=kOutput, calls=%fused_computation.18 | convolution fusion | flops 6446645248 | bytes 16252928 | tf_op jit(solution)/shard_map/dot_general | solution.py:157
  396.5 51.1 %reduce-scatter.3.cloned.1.call-done = bf16[16,8,4096]{2,0,1:T(8,128)(2,1)} async-done(((bf16[128,8,4096]{2,0,1:T(8,128)(2,1)}), bf16[16,8,4096]{2,0,1:T(8,128)(2,1)}) %reduce-scatter.3.cloned.1.call-update) | async-done | bytes 1048592 | tf_op jit(solution)/shard_map/reduce_scatter | solution.py:156
  447.7 2.8 copy.87
  450.4 7.2 %all-to-all-start.1 = ((bf16[16,8,4096]{2,1,0:T(8,128)(2,1)}), bf16[16,8,4096]{2,1,0:T(8,128)(2,1)S(1)}, u32[]{:S(2)}, u32[]{:S(2)}) async-start(bf16[16,8,4096]{2,1,0:T(8,128)(2,1)} %copy.87), calls=%async_computation.2 | async-start | bytes 2097152 | tf_op jit(solution)/shard_map/all_to_all | solution.py:164
  457.9 19.5 %all-to-all-done.1 = bf16[16,8,4096]{2,1,0:T(8,128)(2,1)S(1)} async-done(((bf16[16,8,4096]{2,1,0:T(8,128)(2,1)}), bf16[16,8,4096]{2,1,0:T(8,128)(2,1)S(1)}, u32[]{:S(2)}, u32[]{:S(2)}) %all-to-all-start.1) | async-done | bytes 1048608 | tf_op jit(solution)/shard_map/all_to_all | solution.py:164
  477.5 1.4 fusion.9
  (714 shorter events, 71.6 us)
Async XLA Ops:
  6.5 8.1 %copy-start = (bf16[512,288]{0,1:T(8,128)(2,1)S(1)}, bf16[512,288]{0,1:T(8,128)(2,1)}, u32[]{:S(2)}) copy-start(bf16[512,288]{0,1:T(8,128)(2,1)} %param.27) | copy-start | bytes 884740
  6.5 9.2 %copy-start.3 = (f32[16,512]{1,0:T(8,128)S(1)}, f32[16,512]{1,0:T(8,128)}, u32[]{:S(2)}) copy-start(f32[16,512]{1,0:T(8,128)} %param.30) | copy-start | bytes 98308
  6.5 95.3 %copy-start.2 = (bf16[256,512]{1,0:T(8,128)(2,1)S(1)}, bf16[256,512]{1,0:T(8,128)(2,1)}, u32[]{:S(2)}) copy-start(bf16[256,512]{1,0:T(8,128)(2,1)} %param.28) | copy-start | bytes 786436
  6.5 95.3 %copy-start.6 = (f32[512]{0:T(512)S(1)}, f32[512]{0:T(512)}, u32[]{:S(2)}) copy-start(f32[512]{0:T(512)} %param.29) | copy-start | bytes 6148
  6.5 95.2 %all-reduce.4.cloned.1.call-start = ((), (), s32[]{:S(2)}) async-start(), calls=%async_computation.3 | async-start | bytes 393216 | tf_op jit(solution)/shard_map/psum | solution.py:102
  7.4 5.0 %collective-permute-start = (bf16[3,4,512]{2,1,0:T(4,128)(2,1)S(1)}, bf16[3,4,512]{2,1,0:T(4,128)(2,1)S(1)}, u32[]{:S(2)}, u32[]{:S(2)}) collective-permute-start(bf16[3,4,512]{2,1,0:T(4,128)(2,1)S(1)} %slice.38), channel_id=1, source_target_pairs={{0,16},{16,32},{32,48},{48,64},{64,80},{80,96},{96,112},{1,17},{17... | collective-permute-start | bytes 36872 | tf_op jit(solution)/shard_map/ppermute | solution.py:17
  15.7 281.4 %all-reduce.6.cloned.1.call-start = ((), (), s32[]{:S(2)}) async-start(), calls=%async_computation.6 | async-start | bytes 4194304
  105.3 95.6 %copy-start.7 = (f32[512]{0:T(512)S(1)}, f32[512]{0:T(512)}, u32[]{:S(2)}) copy-start(f32[512]{0:T(512)} %param.31) | copy-start | bytes 6148
  202.3 4.9 %copy-start.5 = (s32[4,4,2]{1,2,0:T(2,128)S(1)}, s32[4,4,2]{1,2,0:T(2,128)}, u32[]{:S(2)}) copy-start(s32[4,4,2]{1,2,0:T(2,128)} %param.35) | copy-start | bytes 388
  202.3 5.7 %copy-start.10 = (u32[128]{0:T(128)S(1)}, u32[128]{0:T(128)}, u32[]{:S(2)}) copy-start(u32[128]{0:T(128)} %constant.77) | copy-start | bytes 1540
  202.3 95.9 %copy-start.1 = (bf16[4,4,4096]{2,1,0:T(4,128)(2,1)S(1)}, bf16[4,4,4096]{2,1,0:T(4,128)(2,1)}, u32[]{:S(2)}) copy-start(bf16[4,4,4096]{2,1,0:T(4,128)(2,1)} %param.33) | copy-start | bytes 393220
  202.3 96.1 %copy-start.4 = (f32[4096]{0:T(1024)S(1)}, f32[4096]{0:T(1024)}, u32[]{:S(2)}) copy-start(f32[4096]{0:T(1024)} %param.34) | copy-start | bytes 49156
  207.1 159.5 %all-gather.3.cloned.1.call-start = ((), (), s32[]{:S(2)}) async-start(), calls=%async_computation.4 | async-start | bytes 9437184 | tf_op jit(solution)/shard_map/all_gather | solution.py:150
  319.7 128.0 %reduce-scatter.3.cloned.1.call-start = ((), (), s32[]{:S(2)}) async-start(), calls=%async_computation.5 | async-start | bytes 9437184 | tf_op jit(solution)/shard_map/reduce_scatter | solution.py:156
  366.6 11.0 %copy-start.9 = (bf16[128,8,4096]{2,1,0:T(8,128)(2,1)S(1)}, bf16[128,8,4096]{2,1,0:T(8,128)(2,1)}, u32[]{:S(2)}) copy-start(bf16[128,8,4096]{2,1,0:T(8,128)(2,1)} %all-gather.3.cloned.1.call-done) | copy-start | bytes 25165828
  366.6 21.0 %slice-start = ((s8[6291456]{0:T(1024)(128)(4,1)}), s8[4194304]{0:T(1024)(128)(4,1)S(1)}, s32[]{:S(2)}) async-start(s8[6291456]{0:T(1024)(128)(4,1)} %bitcast.121), calls=%async_computation.7 | async-start | bytes 8388608
  377.7 10.0 %slice-start.1 = ((s8[6291456]{0:T(1024)(128)(4,1)}), s8[2097152]{0:T(1024)(128)(4,1)S(1)}, s32[]{:S(2)}) async-start(s8[6291456]{0:T(1024)(128)(4,1)} %bitcast.121), calls=%async_computation.8 | async-start | bytes 4194304
  396.5 61.2 %copy-start.8 = (bf16[4,4,2]{1,2,0:T(2,128)(2,1)S(1)}, bf16[4,4,2]{1,2,0:T(2,128)(2,1)}, u32[]{:S(2)}) copy-start(bf16[4,4,2]{1,2,0:T(2,128)(2,1)} %param.36) | copy-start | bytes 196
  450.4 26.9 %all-to-all-start.1 = ((bf16[16,8,4096]{2,1,0:T(8,128)(2,1)}), bf16[16,8,4096]{2,1,0:T(8,128)(2,1)S(1)}, u32[]{:S(2)}, u32[]{:S(2)}) async-start(bf16[16,8,4096]{2,1,0:T(8,128)(2,1)} %copy.87), calls=%async_computation.2 | async-start | bytes 2097152 | tf_op jit(solution)/shard_map/all_to_all | solution.py:164
Sparse Core Ops, SparseCore 0:
  15.8 85.9 all-reduce.3
  207.3 89.8 all-reduce.5
  319.8 46.7 all-gather.2
  396.7 50.9 reduce-scatter.2
where the time goes:
time: 489 us; the launch traced here: 485 us
  waiting for transfers between devices  293 us (60%)
  local copies, waits for them, and re-layouts  58.7 us (12%)
  blocking collectives  46.9 us (10%)
  matrix products  38.5 us (8%)
  other arithmetic  19.2 us (4%)
  between operations  14.1 us (3%)
  starting transfers between devices  9.47 us (2%)
  loops' own time  5.32 us (1%)
    unnamed x5, waiting for transfers between devices  87.8 us
    psum x1, waiting for transfers between devices, per_device(): lax.psum(projected.astype(jnp.bfloat16), 'exp').astype(jnp.float32)  86 us
    reduce_scatter x1, waiting for transfers between devices, per_device(): lax.psum_scatter(jnp.dot(hidden, w_down[0], preferred_element_type=jnp.fl...  51.1 us
    dynamic_slice x64, local copies, waits for them, and re-layouts, per_device(): final_local, local_out = lax.scan(advance, zero_state, series)  47 us
    all_gather x1, waiting for transfers between devices, per_device(): everything = lax.all_gather(arrived, 'seq', axis=0, tiled=True)  46.7 us
    all_gather x2, blocking collectives, entering(): lax.all_gather(a.astype(kind), axis)  26.2 us
    all_to_all x1, blocking collectives, per_device(): lax.all_to_all(jnp.tile(outgoing, (splits, 1, 1)), 'exp', split_axis=0, c...  20.6 us
    all_to_all x1, waiting for transfers between devices, per_device(): lax.all_to_all(own_rows.astype(jnp.bfloat16), 'exp', split_axis=0, concat...  19.5 us
  transfers between devices with their start and end apart: 6, of which 6 were waited for; matrix products, arithmetic and copies ran while one was open for 1% of the time, Pallas kernels for 0%

commit v1 on v0

--- a/solution.py
+++ b/solution.py
@@ -144,9 +144,20 @@
         .astype(jnp.bfloat16)
         .reshape(EXPERTS, capacity, D)
     )
-    arrived = lax.all_to_all(
-        jnp.tile(outgoing, (splits, 1, 1)), "exp", split_axis=0, concat_axis=0, tiled=True
-    )
+    array = jnp.tile(outgoing, (splits, 1, 1))
+    ways, here = (lax.axis_size("exp"), lax.axis_index("exp"))
+    width = array.shape[0] // ways
+    dims = list(array.shape)
+    dims[0] = width
+    height = dims[0]
+    dims[0] = height * ways
+    full = jnp.zeros(dims, array.dtype)
+    for mask in range(ways):
+        part = lax.dynamic_slice_in_dim(array, (here ^ mask) * width, width, axis=0)
+        if mask:
+            part = lax.ppermute(part, "exp", [(d, d ^ mask) for d in range(ways)])
+        full = lax.dynamic_update_slice_in_dim(full, part, (here ^ mask) * height, axis=0)
+    arrived = full
     everything = lax.all_gather(arrived, "seq", axis=0, tiled=True)
     row_block = everything
     expert_row_block = row_block.reshape(-1, D)

time: 489 us -> 553 us (1.13)
  local copies, waits for them, and re-layouts: 58.7 us -> 104 us
  starting transfers between devices: 9.47 us -> 41.5 us
  blocking collectives: 46.9 us -> 26.2 us
  waiting for transfers between devices: 293 us -> 299 us
    mul x128, local copies, waits for them, and re-layouts: 0.74 us -> 43.6 us  [advance(): (step_now * value_now)[:, None, :] * input_now[:, :, None]]
    ppermute x0 -> x15, starting transfers between devices: none -> 32.1 us  [per_device(): part = lax.ppermute(part, 'exp', [(d, d ^ mask) for d in range(ways)])]
    all_to_all x1 -> x0, blocking collectives: 20.6 us -> none  [per_device(): lax.all_to_all(jnp.tile(outgoing, (splits, 1, 1)), 'exp', split_axis=0, c...]
  transfers between devices with their start and end apart: 6 -> 21, of which waited for: 6 -> 8; matrix products, arithmetic and copies ran while one was open for 1% -> 0% of each run, Pallas kernels for 0% -> 0%
where the time goes in v1:
time: 553 us; the launch traced here: 547 us
  waiting for transfers between devices  299 us (54%)
  local copies, waits for them, and re-layouts  104 us (19%)
  starting transfers between devices  41.5 us (8%)
  matrix products  38.4 us (7%)
  blocking collectives  26.2 us (5%)
  other arithmetic  19.1 us (3%)
  between operations  14.5 us (3%)
    unnamed x5, waiting for transfers between devices  87.6 us
    psum x1, waiting for transfers between devices, per_device(): lax.psum(projected.astype(jnp.bfloat16), 'exp').astype(jnp.float32)  86.1 us
    reduce_scatter x1, waiting for transfers between devices, per_device(): lax.psum_scatter(jnp.dot(hidden, w_down[0], preferred_element_type=jnp.fl...  51.1 us
    dynamic_slice x64, local copies, waits for them, and re-layouts, per_device(): final_local, local_out = lax.scan(advance, zero_state, series)  47 us
    all_gather x1, waiting for transfers between devices, per_device(): everything = lax.all_gather(arrived, 'seq', axis=0, tiled=True)  46.9 us
    mul x128, local copies, waits for them, and re-layouts, advance(): (step_now * value_now)[:, None, :] * input_now[:, :, None]  43.6 us
    ppermute x15, starting transfers between devices, per_device(): part = lax.ppermute(part, 'exp', [(d, d ^ mask) for d in range(ways)])  32.1 us
    all_gather x2, blocking collectives, entering(): lax.all_gather(a.astype(kind), axis)  26.2 us
  transfers between devices with their start and end apart: 21, of which 8 were waited for; matrix products, arithmetic and copies ran while one was open for 0% of the time, Pallas kernels for 0%

profile of v1, /device:TPU:2, one launch (start us, length us, event | category | flops | bytes accessed | tf_op | source)
XLA Modules:
  0.0 547.3 jit_solution(12201401580831395840)
XLA Ops:
  10.2 2.2 collective-permute-done
  15.8 86.1 %all-reduce.4.cloned.1.call-done = bf16[64,4,288]{2,0,1:T(8,128)(2,1)} async-done(((bf16[64,4,288]{2,0,1:T(8,128)(2,1)}), bf16[64,4,288]{2,0,1:T(8,128)(2,1)}) %all-reduce.4.cloned.1.call-update) | async-done | bytes 147472 | tf_op jit(solution)/shard_map/psum | solution.py:102
  105.4 10.3 %while.37 = (s32[]{:T(128)}, f32[4,16,512]{2,1,0:T(8,128)S(1)}, f32[64,4,512]{2,1,0:T(4,128)S(1)}, f32[16,512]{1,0:T(8,128)S(1)}, f32[64,4,512]{2,1,0:T(4,128)S(...) while((s32[]{:T(128)}, f32[4,16,512]{2,1,0:T(8,128)S(1)}, f32[64,4,512]{2,1,0:T(4,128)S(1)}, ...), condition=%wide.region_3.4_spmd.clone, body=%wide.region_2.3_spmd.clone.sunk | while | flops 165891 | bytes 353131 | solution.py:114
  116.4 13.1 %all-gather = bf16[32,16,512]{2,1,0:T(8,128)(2,1)S(1)} all-gather(bf16[4,16,512]{2,1,0:T(8,128)(2,1)S(1)} %convert_element_type.103), channel_id=2, replica_groups=mesh['seq'=8,'exp'=16] {'seq'}, dimensions={0}, use_global_device_ids=true | all-gather | bytes 589824 | tf_op jit(solution)/shard_map/all_gather | solution.py:23
  129.5 13.1 %all_gather.13 = bf16[8,4,16,512]{3,2,1,0:T(8,128)(2,1)S(1)} all-gather(bf16[1,4,16,512]{3,2,1,0:T(8,128)(2,1)S(1)} %exponential_convert_fusion), channel_id=1, replica_groups=mesh['seq'=8,'exp'=16] {'seq'}, dimensions={0}, use_global_device_ids=true | all-gather | bytes 589824 | tf_op jit(solution)/shard_map/all_gather | solution.py:23
  142.8 101.5 %while.36 = (s32[]{:T(128)}, f32[4,16,512]{2,1,0:T(8,128)S(1)}, f32[64,4,512]{2,1,0:T(4,128)S(1)}, f32[64,4,512]{2,1,0:T(4,128)S(1)}, f32[16,512]{1,0:T(8,128)S(...) while((s32[]{:T(128)}, f32[4,16,512]{2,1,0:T(8,128)S(1)}, ...), condition=%wide.region_8.9_spmd, body=%wide.region_6.8_spmd.sunk | while | flops 196610 | bytes 378481 | solution.py:118
  245.8 4.8 convolution_convert_fusion.1
  253.0 87.6 %all-reduce.6.cloned.1.call-done = bf16[64,4,4096]{2,0,1:T(8,128)(2,1)} async-done(((bf16[64,4,4096]{2,0,1:T(8,128)(2,1)}), bf16[64,4,4096]{2,0,1:T(8,128)(2,1)}) %all-reduce.6.cloned.1.call-update) | async-done | bytes 2097168
  344.1 2.7 collective-permute-start.2
  349.0 3.5 collective-permute-start.6
  356.8 6.0 %collective-permute-start.10 = (bf16[1,8,4096]{2,1,0:T(8,128)(2,1)S(1)}, bf16[1,8,4096]{2,1,0:T(8,128)(2,1)S(1)}, u32[]{:S(2)}, u32[]{:S(2)}) collective-permute-start(bf16[1,8,4096]{2,1,0:T(8,128)(2,1)S(1)} %get-tuple-element.252), channel_id=1, source_target_pairs={{0,10},{1,11},{2,8},{3,9},{4,14},{5,15},{6,12},{7,13},{8,2},{9,3},... | collective-permute-start | bytes 196616 | tf_op jit(solution)/shard_map/ppermute | solution.py:158
  362.9 2.3 collective-permute-start.11
  365.2 2.5 collective-permute-start.12
  367.9 4.7 collective-permute-start.14
  372.6 2.5 collective-permute-start.15
  375.9 4.4 collective-permute-done.15
  381.6 46.9 %all-gather.3.cloned.1.call-done = bf16[128,8,4096]{2,1,0:T(8,128)(2,1)} async-done(((bf16[16,8,4096]{2,1,0:T(8,128)(2,1)}), bf16[128,8,4096]{2,1,0:T(8,128)(2,1)}) %all-gather.3.cloned.1.call-update) | async-done | bytes 8388624 | tf_op jit(solution)/shard_map/all_gather | solution.py:161
  428.5 11.0 %fusion.3 = f32[1024,768]{1,0:T(8,128)S(1)} fusion(bf16[128,8,4096]{2,1,0:T(8,128)(2,1)} %all-gather.3.cloned.1.call-done, bf16[1,4096,768]{2,1,0:T(8,128)(2,1)} %param.37), kind=kOutput, calls=%fused_computation.16 | convolution fusion | flops 6442450944 | bytes 17825792 | tf_op jit(solution)/shard_map/dot_general | solution.py:164
  439.6 9.9 %fusion.12 = bf16[128,8,768]{2,1,0:T(8,128)(2,1)S(1)} fusion(f32[1024,768]{1,0:T(8,128)S(1)} %fusion.3, bf16[1,4096,768]{2,1,0:T(8,128)(2,1)} %param.38, bf16[128,8,4096]{2,1,0:T(8,128)(2,1)S(1)} %copy-done.11), kind=kOutput, calls=%fused_computation.31 | convolution fusion | flops 6447169536 | bytes 19398656 | tf_op jit(solution)/shard_map/dot_general | solution.py:165
  449.5 8.9 %convolution_convert_fusion = bf16[128,8,4096]{2,0,1:T(8,128)(2,1)} fusion(bf16[1,768,4096]{2,1,0:T(8,128)(2,1)S(1)} %bitcast.118, bf16[128,8,768]{2,1,0:T(8,128)(2,1)S(1)} %fusion.12), kind=kOutput, calls=%fused_computation.18 | convolution fusion | flops 6446645248 | bytes 16252928 | tf_op jit(solution)/shard_map/dot_general | solution.py:168
  458.4 51.1 %reduce-scatter.3.cloned.1.call-done = bf16[16,8,4096]{2,0,1:T(8,128)(2,1)} async-done(((bf16[128,8,4096]{2,0,1:T(8,128)(2,1)}), bf16[16,8,4096]{2,0,1:T(8,128)(2,1)}) %reduce-scatter.3.cloned.1.call-update) | async-done | bytes 1048592 | tf_op jit(solution)/shard_map/reduce_scatter | solution.py:167
  509.5 2.8 copy.87
  512.3 7.2 %all-to-all-start = ((bf16[16,8,4096]{2,1,0:T(8,128)(2,1)}), bf16[16,8,4096]{2,1,0:T(8,128)(2,1)S(1)}, u32[]{:S(2)}, u32[]{:S(2)}) async-start(bf16[16,8,4096]{2,1,0:T(8,128)(2,1)} %copy.87), calls=%async_computation.1 | async-start | bytes 2097152 | tf_op jit(solution)/shard_map/all_to_all | solution.py:175
  519.7 19.5 %all-to-all-done = bf16[16,8,4096]{2,1,0:T(8,128)(2,1)S(1)} async-done(((bf16[16,8,4096]{2,1,0:T(8,128)(2,1)}), bf16[16,8,4096]{2,1,0:T(8,128)(2,1)S(1)}, u32[]{:S(2)}, u32[]{:S(2)}) %all-to-all-start) | async-done | bytes 1048608 | tf_op jit(solution)/shard_map/all_to_all | solution.py:175
  (764 shorter events, 134.9 us)
Async XLA Ops:
  6.5 95.3 %all-reduce.4.cloned.1.call-start = ((), (), s32[]{:S(2)}) async-start(), calls=%async_computation.2 | async-start | bytes 393216 | tf_op jit(solution)/shard_map/psum | solution.py:102
  7.4 5.0 collective-permute-start
  15.7 324.9 %all-reduce.6.cloned.1.call-start = ((), (), s32[]{:S(2)}) async-start(), calls=%async_computation.5 | async-start | bytes 4194304
  105.3 139.1 %copy-start.9 = (f32[512]{0:T(512)S(1)}, f32[512]{0:T(512)}, u32[]{:S(2)}) copy-start(f32[512]{0:T(512)} %param.31) | copy-start | bytes 6148
  245.8 95.8 %copy-start.2 = (bf16[4,4,4096]{2,1,0:T(4,128)(2,1)S(1)}, bf16[4,4,4096]{2,1,0:T(4,128)(2,1)}, u32[]{:S(2)}) copy-start(bf16[4,4,4096]{2,1,0:T(4,128)(2,1)} %param.33) | copy-start | bytes 393220
  245.8 96.1 %copy-start.6 = (f32[4096]{0:T(1024)S(1)}, f32[4096]{0:T(1024)}, u32[]{:S(2)}) copy-start(f32[4096]{0:T(1024)} %param.34) | copy-start | bytes 49156
  250.6 177.9 %all-gather.3.cloned.1.call-start = ((), (), s32[]{:S(2)}) async-start(), calls=%async_computation.3 | async-start | bytes 9437184 | tf_op jit(solution)/shard_map/all_gather | solution.py:161
  342.8 6.3 %collective-permute-start.1 = (bf16[1,8,4096]{2,1,0:T(8,128)(2,1)S(1)}, bf16[1,8,4096]{2,1,0:T(8,128)(2,1)S(1)}, u32[]{:S(2)}, u32[]{:S(2)}) collective-permute-start(bf16[1,8,4096]{2,1,0:T(8,128)(2,1)S(1)} %get-tuple-element.261), channel_id=1, source_target_pairs={{0,1},{1,0},{2,3},{3,2},{4,5},{5,4},{6,7},{7,6},{8,9},{9,8},{10,11... | collective-permute-start | bytes 196616 | tf_op jit(solution)/shard_map/ppermute | solution.py:158
  344.1 8.4 %collective-permute-start.2 = (bf16[1,8,4096]{2,1,0:T(8,128)(2,1)S(1)}, bf16[1,8,4096]{2,1,0:T(8,128)(2,1)S(1)}, u32[]{:S(2)}, u32[]{:S(2)}) collective-permute-start(bf16[1,8,4096]{2,1,0:T(8,128)(2,1)S(1)} %get-tuple-element.260), channel_id=1, source_target_pairs={{0,2},{1,3},{2,0},{3,1},{4,6},{5,7},{6,4},{7,5},{8,10},{9,11},{10,... | collective-permute-start | bytes 196616 | tf_op jit(solution)/shard_map/ppermute | solution.py:158
  346.8 8.0 %collective-permute-start.3 = (bf16[1,8,4096]{2,1,0:T(8,128)(2,1)S(1)}, bf16[1,8,4096]{2,1,0:T(8,128)(2,1)S(1)}, u32[]{:S(2)}, u32[]{:S(2)}) collective-permute-start(bf16[1,8,4096]{2,1,0:T(8,128)(2,1)S(1)} %get-tuple-element.259), channel_id=1, source_target_pairs={{0,3},{1,2},{2,1},{3,0},{4,7},{5,6},{6,5},{7,4},{8,11},{9,10},{10,... | collective-permute-start | bytes 196616 | tf_op jit(solution)/shard_map/ppermute | solution.py:158
  347.5 9.2 %collective-permute-start.4 = (bf16[1,8,4096]{2,1,0:T(8,128)(2,1)S(1)}, bf16[1,8,4096]{2,1,0:T(8,128)(2,1)S(1)}, u32[]{:S(2)}, u32[]{:S(2)}) collective-permute-start(bf16[1,8,4096]{2,1,0:T(8,128)(2,1)S(1)} %get-tuple-element.258), channel_id=1, source_target_pairs={{0,4},{1,5},{2,6},{3,7},{4,0},{5,1},{6,2},{7,3},{8,12},{9,13},{10,... | collective-permute-start | bytes 196616 | tf_op jit(solution)/shard_map/ppermute | solution.py:158
  348.8 8.1 %collective-permute-start.5 = (bf16[1,8,4096]{2,1,0:T(8,128)(2,1)S(1)}, bf16[1,8,4096]{2,1,0:T(8,128)(2,1)S(1)}, u32[]{:S(2)}, u32[]{:S(2)}) collective-permute-start(bf16[1,8,4096]{2,1,0:T(8,128)(2,1)S(1)} %get-tuple-element.257), channel_id=1, source_target_pairs={{0,5},{1,4},{2,7},{3,6},{4,1},{5,0},{6,3},{7,2},{8,13},{9,12},{10,... | collective-permute-start | bytes 196616 | tf_op jit(solution)/shard_map/ppermute | solution.py:158
  349.0 13.8 %collective-permute-start.6 = (bf16[1,8,4096]{2,1,0:T(8,128)(2,1)S(1)}, bf16[1,8,4096]{2,1,0:T(8,128)(2,1)S(1)}, u32[]{:S(2)}, u32[]{:S(2)}) collective-permute-start(bf16[1,8,4096]{2,1,0:T(8,128)(2,1)S(1)} %get-tuple-element.256), channel_id=1, source_target_pairs={{0,6},{1,7},{2,4},{3,5},{4,2},{5,3},{6,0},{7,1},{8,14},{9,15},{10,... | collective-permute-start | bytes 196616 | tf_op jit(solution)/shard_map/ppermute | solution.py:158
  352.5 12.7 %collective-permute-start.7 = (bf16[1,8,4096]{2,1,0:T(8,128)(2,1)S(1)}, bf16[1,8,4096]{2,1,0:T(8,128)(2,1)S(1)}, u32[]{:S(2)}, u32[]{:S(2)}) collective-permute-start(bf16[1,8,4096]{2,1,0:T(8,128)(2,1)S(1)} %get-tuple-element.255), channel_id=1, source_target_pairs={{0,7},{1,6},{2,5},{3,4},{4,3},{5,2},{6,1},{7,0},{8,15},{9,14},{10,... | collective-permute-start | bytes 196616 | tf_op jit(solution)/shard_map/ppermute | solution.py:158
  354.7 13.0 %collective-permute-start.8 = (bf16[1,8,4096]{2,1,0:T(8,128)(2,1)S(1)}, bf16[1,8,4096]{2,1,0:T(8,128)(2,1)S(1)}, u32[]{:S(2)}, u32[]{:S(2)}) collective-permute-start(bf16[1,8,4096]{2,1,0:T(8,128)(2,1)S(1)} %get-tuple-element.254), channel_id=1, source_target_pairs={{0,8},{1,9},{2,10},{3,11},{4,12},{5,13},{6,14},{7,15},{8,0},{9,1},... | collective-permute-start | bytes 196616 | tf_op jit(solution)/shard_map/ppermute | solution.py:158
  356.7 11.2 %collective-permute-start.9 = (bf16[1,8,4096]{2,1,0:T(8,128)(2,1)S(1)}, bf16[1,8,4096]{2,1,0:T(8,128)(2,1)S(1)}, u32[]{:S(2)}, u32[]{:S(2)}) collective-permute-start(bf16[1,8,4096]{2,1,0:T(8,128)(2,1)S(1)} %get-tuple-element.253), channel_id=1, source_target_pairs={{0,9},{1,8},{2,11},{3,10},{4,13},{5,12},{6,15},{7,14},{8,1},{9,0},... | collective-permute-start | bytes 196616 | tf_op jit(solution)/shard_map/ppermute | solution.py:158
  356.8 15.7 %collective-permute-start.10 = (bf16[1,8,4096]{2,1,0:T(8,128)(2,1)S(1)}, bf16[1,8,4096]{2,1,0:T(8,128)(2,1)S(1)}, u32[]{:S(2)}, u32[]{:S(2)}) collective-permute-start(bf16[1,8,4096]{2,1,0:T(8,128)(2,1)S(1)} %get-tuple-element.252), channel_id=1, source_target_pairs={{0,10},{1,11},{2,8},{3,9},{4,14},{5,15},{6,12},{7,13},{8,2},{9,3},... | collective-permute-start | bytes 196616 | tf_op jit(solution)/shard_map/ppermute | solution.py:158
  362.9 12.2 %collective-permute-start.11 = (bf16[1,8,4096]{2,1,0:T(8,128)(2,1)S(1)}, bf16[1,8,4096]{2,1,0:T(8,128)(2,1)S(1)}, u32[]{:S(2)}, u32[]{:S(2)}) collective-permute-start(bf16[1,8,4096]{2,1,0:T(8,128)(2,1)S(1)} %get-tuple-element.251), channel_id=1, source_target_pairs={{0,11},{1,10},{2,9},{3,8},{4,15},{5,14},{6,13},{7,12},{8,3},{9,2},... | collective-permute-start | bytes 196616 | tf_op jit(solution)/shard_map/ppermute | solution.py:158
  365.2 9.9 %collective-permute-start.12 = (bf16[1,8,4096]{2,1,0:T(8,128)(2,1)S(1)}, bf16[1,8,4096]{2,1,0:T(8,128)(2,1)S(1)}, u32[]{:S(2)}, u32[]{:S(2)}) collective-permute-start(bf16[1,8,4096]{2,1,0:T(8,128)(2,1)S(1)} %get-tuple-element.250), channel_id=1, source_target_pairs={{0,12},{1,13},{2,14},{3,15},{4,8},{5,9},{6,10},{7,11},{8,4},{9,5},... | collective-permute-start | bytes 196616 | tf_op jit(solution)/shard_map/ppermute | solution.py:158
  367.8 7.4 %collective-permute-start.13 = (bf16[1,8,4096]{2,1,0:T(8,128)(2,1)S(1)}, bf16[1,8,4096]{2,1,0:T(8,128)(2,1)S(1)}, u32[]{:S(2)}, u32[]{:S(2)}) collective-permute-start(bf16[1,8,4096]{2,1,0:T(8,128)(2,1)S(1)} %get-tuple-element.249), channel_id=1, source_target_pairs={{0,13},{1,12},{2,15},{3,14},{4,9},{5,8},{6,11},{7,10},{8,5},{9,4},... | collective-permute-start | bytes 196616 | tf_op jit(solution)/shard_map/ppermute | solution.py:158
  367.9 8.0 %collective-permute-start.14 = (bf16[1,8,4096]{2,1,0:T(8,128)(2,1)S(1)}, bf16[1,8,4096]{2,1,0:T(8,128)(2,1)S(1)}, u32[]{:S(2)}, u32[]{:S(2)}) collective-permute-start(bf16[1,8,4096]{2,1,0:T(8,128)(2,1)S(1)} %get-tuple-element.248), channel_id=1, source_target_pairs={{0,14},{1,15},{2,12},{3,13},{4,10},{5,11},{6,8},{7,9},{8,6},{9,7},... | collective-permute-start | bytes 196616 | tf_op jit(solution)/shard_map/ppermute | solution.py:158
  372.6 7.7 %collective-permute-start.15 = (bf16[1,8,4096]{2,1,0:T(8,128)(2,1)S(1)}, bf16[1,8,4096]{2,1,0:T(8,128)(2,1)S(1)}, u32[]{:S(2)}, u32[]{:S(2)}) collective-permute-start(bf16[1,8,4096]{2,1,0:T(8,128)(2,1)S(1)} %get-tuple-element.247), channel_id=1, source_target_pairs={{0,15},{1,14},{2,13},{3,12},{4,11},{5,10},{6,9},{7,8},{8,7},{9,6},... | collective-permute-start | bytes 196616 | tf_op jit(solution)/shard_map/ppermute | solution.py:158
  381.4 128.1 %reduce-scatter.3.cloned.1.call-start = ((), (), s32[]{:S(2)}) async-start(), calls=%async_computation.4 | async-start | bytes 9437184 | tf_op jit(solution)/shard_map/reduce_scatter | solution.py:167
  512.3 26.9 %all-to-all-start = ((bf16[16,8,4096]{2,1,0:T(8,128)(2,1)}), bf16[16,8,4096]{2,1,0:T(8,128)(2,1)S(1)}, u32[]{:S(2)}, u32[]{:S(2)}) async-start(bf16[16,8,4096]{2,1,0:T(8,128)(2,1)} %copy.87), calls=%async_computation.1 | async-start | bytes 2097152 | tf_op jit(solution)/shard_map/all_to_all | solution.py:175
  (12 other events, 323.4 us)
Sparse Core Ops, SparseCore 0:
  15.8 85.9 all-reduce.3
  250.7 89.7 all-reduce.5
  381.5 46.9 all-gather.2
  458.5 50.9 reduce-scatter.2
